TPU v7x, 32 devices: a whole 2x2x4 slice. The times are simulated.
32 devices in a mesh: row: 8 (over z, core), col: 4 (over y, x).
Axes of the slice: x: 2, y: 2, z: 4, core: 2. Of those that a mesh axis runs over, the one named last changes fastest.
Arguments:
- gram: bfloat16 [32768, 32768], P('row', 'col'), may hold values from -1 to 5, as said below
- start_basis: bfloat16 [32768, 256], P(('row', 'col')), may hold values from -12 to 12
- slab: float32 [32768, 4096], P('row', 'col'), may hold values from -6 to 6
Outputs:
- core_scaled: float32 [32768, 256], P(('row', 'col'))
- next_unfolding: float32 [4096, 256], P(('row', 'col'))
Inputs may be any that keep to these rules, and one draw needn't show every extreme that they name: gram is symmetric: entry (i, j) equals entry (j, i).
All inputs are finite; a program needn't handle non-finite values.
Results may differ from a plain program's by a relative error of at most 0.003.
Values may be sent and summed in bfloat16 or wider, within the bound.
A program may use at most 192 MiB of HBM per device.

v0:
```python
import math
import jax
import jax.numpy as jnp
from jax import lax
from jax.sharding import PartitionSpec as P

N = 32768
NMODE = 16


def body(gram, start_basis, slab):
    col_count = lax.axis_size("col")
    highest = lax.Precision.HIGHEST
    contract_rows = (((0,), (0,)), ((), ()))
    own_rows = lax.all_gather(start_basis, "col", axis=0, tiled=True)
    first_image = lax.psum_scatter(
        lax.dot_general(gram, own_rows, contract_rows, preferred_element_type=jnp.float32),
        "row",
        scatter_dimension=0,
        tiled=True,
    ).astype(jnp.bfloat16)
    col_rows = lax.all_gather(first_image, "row", axis=0, tiled=True)
    second_image = lax.psum_scatter(
        jnp.dot(gram, col_rows, preferred_element_type=jnp.float32),
        "col",
        scatter_dimension=0,
        tiled=True,
    )
    own_gram = lax.dot_general(
        second_image,
        second_image,
        contract_rows,
        precision=highest,
        preferred_element_type=jnp.float32,
    )
    small_gram = lax.psum(own_gram, ("row", "col"))
    factor = jnp.linalg.cholesky(small_gram)
    basis_cols = jax.scipy.linalg.solve_triangular(factor, second_image.T, lower=True).T
    block_basis = lax.all_gather(basis_cols, "col", axis=0, tiled=True)
    own_proj = lax.psum_scatter(
        lax.dot_general(
            block_basis, slab, contract_rows, precision=highest, preferred_element_type=jnp.float32
        ),
        "row",
        scatter_dimension=0,
        tiled=True,
    )
    core_out = basis_cols * math.sqrt(N)
    mode_share = NMODE // col_count
    grouped = own_proj.reshape(own_proj.shape[0], mode_share, own_proj.shape[1] // mode_share)
    regrouped = lax.all_to_all(grouped, "col", split_axis=0, concat_axis=1, tiled=True)
    return (
        core_out,
        regrouped.reshape(regrouped.shape[0] * regrouped.shape[1], regrouped.shape[2]),
    )


def solution(mesh):
    in_specs = (P("row", "col"), P(("row", "col"), None), P("row", "col"))
    out_specs = (P(("row", "col"), None), P(("row", "col"), None))
    return jax.shard_map(body, mesh=mesh, in_specs=in_specs, out_specs=out_specs, check_vma=False)
```

profile of v0, /device:TPU:0, one launch (start us, length us, event | category | flops | bytes accessed | tf_op | source)
XLA Modules:
  0.0 614.0 jit_solution(10611750755675535246)
XLA Ops:
  7.2 0.7 all-gather.4.cloned.1.call-update
  7.9 39.8 %all-gather.4.cloned.1.call-done = bf16[4096,256]{1,0:T(8,128)(2,1)} async-done(((bf16[1024,256]{1,0:T(8,128)(2,1)}), bf16[4096,256]{1,0:T(8,128)(2,1)}) %all-gather.4.cloned.1.call-update) | async-done | bytes 2097168 | tf_op jit(solution)/shard_map/all_gather | solution.py:15
  47.8 30.0 %fusion.9 = f32[8192,256]{1,0:T(8,128)} fusion(bf16[4096,8192]{1,0:T(8,128)(2,1)} %param.3, bf16[4096,256]{1,0:T(8,128)(2,1)} %all-gather.4.cloned.1.call-done), kind=kOutput, calls=%fused_computation.32 | convolution fusion | flops 17179869184 | bytes 77594624 | tf_op jit(solution)/shard_map/dot_general | solution.py:17
  77.8 89.6 %reduce-scatter.4.cloned.1.call-done = f32[1024,256]{1,0:T(8,128)} async-done(((f32[8192,256]{1,0:T(8,128)}), f32[1024,256]{1,0:T(8,128)}) %reduce-scatter.4.cloned.1.call-update) | async-done | bytes 1048592 | tf_op jit(solution)/shard_map/reduce_scatter | solution.py:16
  167.4 2.1 convert_element_type.3
  169.6 45.4 %all-gather.6.cloned.1.call-done = bf16[8192,256]{1,0:T(8,128)(2,1)} async-done(((bf16[1024,256]{1,0:T(8,128)(2,1)}), bf16[8192,256]{1,0:T(8,128)(2,1)}) %all-gather.6.cloned.1.call-update) | async-done | bytes 4194320 | tf_op jit(solution)/shard_map/all_gather | solution.py:22
  215.0 29.2 %convolution_bitcast_fusion = f32[4096,256]{0,1:T(8,128)} fusion(bf16[8192,256]{1,0:T(8,128)(2,1)} %all-gather.6.cloned.1.call-done, bf16[4096,8192]{1,0:T(8,128)(2,1)} %param.3), kind=kOutput, calls=%fused_computation.2 | convolution fusion | flops 17179869184 | bytes 75497472 | tf_op jit(solution)/shard_map/dot_general | solution.py:24
  244.3 51.5 %reduce-scatter.6.cloned.1.call-done = f32[1024,256]{0,1:T(8,128)} async-done(((f32[4096,256]{0,1:T(8,128)}), f32[1024,256]{0,1:T(8,128)}) %reduce-scatter.6.cloned.1.call-update) | async-done | bytes 1048592 | tf_op jit(solution)/shard_map/reduce_scatter | solution.py:23
  295.8 3.4 fusion.10
  299.4 128.9 %all-reduce.3.cloned.1.call-done = f32[256,256]{0,1:T(8,128)} async-done(((f32[256,256]{0,1:T(8,128)}), f32[256,256]{0,1:T(8,128)}) %all-reduce.3.cloned.1.call-update) | async-done | bytes 262160 | tf_op jit(solution)/shard_map/psum | solution.py:36
  428.3 1.1 copy.6
  429.4 1.0 fusion.2
  430.4 11.7 %cholesky.50 = f32[128,128]{1,0:T(8,128)S(1)} custom-call(f32[128,128]{1,0:T(8,128)S(1)} %cholesky.118), custom_call_target="Cholesky" | custom-call | tf_op jit(solution)/shard_map/jit(cholesky)/cholesky | solution.py:37
  442.1 9.8 %custom-call.15 = f32[1,128,128]{1,2,0:T(8,128)S(1)} custom-call(f32[1,128,128]{2,1,0:T(8,128)S(1)} %get-tuple-element.25), custom_call_target="InvertDiagBlocksLowerTriangular" | custom-call | tf_op jit(solution)/shard_map/jit(cholesky)/cholesky | solution.py:37
  452.4 11.7 %cholesky.105 = f32[128,128]{1,0:T(8,128)S(1)} custom-call(f32[128,128]{1,0:T(8,128)S(1)} %convolution_subtract_fusion.1), custom_call_target="Cholesky" | custom-call | tf_op jit(solution)/shard_map/jit(cholesky)/cholesky | solution.py:37
  464.2 0.7 compare_reduce_fusion
  466.4 4.3 while.1
  467.1 1.4 bitcast_dynamic-update-slice_fusion.2
  468.6 0.6 fusion.25
  469.2 1.4 bitcast_dynamic-update-slice_fusion.2
  470.6 19.7 %custom-call.16 = f32[2,128,128]{1,2,0:T(8,128)S(1)} custom-call(f32[2,128,128]{2,1,0:T(8,128)S(1)} %get-tuple-element.9), custom_call_target="InvertDiagBlocksLowerTriangular" | custom-call | tf_op jit(solution)/shard_map/jit(_solve_triangular)/triangular_solve | solution.py:38
  490.3 0.6 fusion
  491.6 0.6 fusion.4
  492.2 1.0 maximum_bitcast_fusion
  493.3 51.7 %all-gather.8.cloned.1.call-done = f32[4096,256]{0,1:T(8,128)} async-done(((f32[1024,256]{0,1:T(8,128)}), f32[4096,256]{0,1:T(8,128)}) %all-gather.8.cloned.1.call-update) | async-done | bytes 4194320 | tf_op jit(solution)/shard_map/all_gather | solution.py:39
  545.1 18.3 %fusion.11 = f32[256,1024]{1,0:T(8,128)} fusion(f32[4096,256]{0,1:T(8,128)} %all-gather.8.cloned.1.call-done, f32[4096,1024]{1,0:T(8,128)} %param.5), kind=kOutput, calls=%fused_computation.34 | convolution fusion | flops 12884901888 | bytes 22020096 | tf_op jit(solution)/shard_map/dot_general | solution.py:41
  563.3 32.8 %reduce-scatter.8.cloned.1.call-done = f32[32,1024]{1,0:T(8,128)} async-done(((f32[256,1024]{1,0:T(8,128)}), f32[32,1024]{1,0:T(8,128)}) %reduce-scatter.8.cloned.1.call-update) | async-done | bytes 131088 | tf_op jit(solution)/shard_map/reduce_scatter | solution.py:40
  596.1 1.6 reshape.30
  597.7 3.7 all-to-all-start
  601.5 1.3 copy.8
  602.9 3.6 all-to-all-done
  606.4 0.7 reshape.31
  (31 shorter events, 2.6 us)
Async XLA Ops:
  7.2 40.6 %all-gather.4.cloned.1.call-start = ((), (), s32[]{:S(2)}) async-start(), calls=%async_computation.4 | async-start | bytes 2621440 | tf_op jit(solution)/shard_map/all_gather | solution.py:15
  7.9 159.5 %reduce-scatter.4.cloned.1.call-start = ((), (), s32[]{:S(2)}) async-start(), calls=%async_computation.5 | async-start | bytes 9437184 | tf_op jit(solution)/shard_map/reduce_scatter | solution.py:16
  77.7 137.3 %all-gather.6.cloned.1.call-start = ((), (), s32[]{:S(2)}) async-start(), calls=%async_computation.6 | async-start | bytes 4718592 | tf_op jit(solution)/shard_map/all_gather | solution.py:22
  169.5 126.2 %reduce-scatter.6.cloned.1.call-start = ((), (), s32[]{:S(2)}) async-start(), calls=%async_computation.7 | async-start | bytes 5242880 | tf_op jit(solution)/shard_map/reduce_scatter | solution.py:23
  244.2 184.1 %all-reduce.3.cloned.1.call-start = ((), (), s32[]{:S(2)}) async-start(), calls=%async_computation.8 | async-start | bytes 524288 | tf_op jit(solution)/shard_map/psum | solution.py:36
  295.8 194.6 %copy-start = (f32[1024,256]{0,1:T(8,128)S(1)}, f32[1024,256]{0,1:T(8,128)}, u32[]{:S(2)}) copy-start(f32[1024,256]{0,1:T(8,128)} %reduce-scatter.6.cloned.1.call-done) | copy-start | bytes 3145732
  299.1 245.9 %all-gather.8.cloned.1.call-start = ((), (), s32[]{:S(2)}) async-start(), calls=%async_computation.9 | async-start | bytes 5242880 | tf_op jit(solution)/shard_map/all_gather | solution.py:39
  493.3 102.9 %reduce-scatter.8.cloned.1.call-start = ((), (), s32[]{:S(2)}) async-start(), calls=%async_computation.10 | async-start | bytes 1179648 | tf_op jit(solution)/shard_map/reduce_scatter | solution.py:40
  597.7 8.7 %all-to-all-start = ((f32[32,4,256]{2,1,0:T(4,128)}), f32[32,4,256]{2,1,0:T(4,128)S(1)}, u32[]{:S(2)}, u32[]{:S(2)}) async-start(f32[32,4,256]{2,1,0:T(4,128)} %reshape.30), calls=%async_computation.3 | async-start | bytes 262144 | tf_op jit(solution)/shard_map/all_to_all | solution.py:51
Sparse Core Ops, SparseCore 0:
  9.8 37.8 all-gather.3
  77.9 89.5 reduce-scatter.3
  169.6 45.3 all-gather.5
  244.3 51.3 reduce-scatter.5
  301.7 126.5 all-reduce.2
  493.4 51.6 all-gather.7
  563.5 32.6 reduce-scatter.7
where the time goes:
time: 614 us
  waiting for transfers between devices  444 us (72%)
  matrix products  83.1 us (14%)
  other arithmetic  58 us (9%)
  between operations  15.6 us (3%)
  local copies, waits for them, and re-layouts  8.87 us (1%)
    psum x1, waiting for transfers between devices, body(): small_gram = lax.psum(own_gram, ('row', 'col'))  129 us
    reduce_scatter x1, waiting for transfers between devices, body(): lax.psum_scatter(lax.dot_general(gram, own_rows, contract_rows, preferred...  89.6 us
    all_gather x1, waiting for transfers between devices, body(): block_basis = lax.all_gather(basis_cols, 'col', axis=0, tiled=True)  51.7 us
    reduce_scatter x1, waiting for transfers between devices, body(): lax.psum_scatter(jnp.dot(gram, col_rows, preferred_element_type=jnp.float...  51.5 us
    all_gather x1, waiting for transfers between devices, body(): col_rows = lax.all_gather(first_image, 'row', axis=0, tiled=True)  45.4 us
    all_gather x1, waiting for transfers between devices, body(): own_rows = lax.all_gather(start_basis, 'col', axis=0, tiled=True)  39.8 us
    another operation x6, other arithmetic, body(): factor = jnp.linalg.cholesky(small_gram)  34 us
    reduce_scatter x1, waiting for transfers between devices, body(): lax.psum_scatter(lax.dot_general(block_basis, slab, contract_rows, precis...  32.8 us
  transfers between devices with their start and end apart: 8, of which 8 were waited for; matrix products, arithmetic and copies ran while one was open for 0% of the time, Pallas kernels for 0%

commit v1 on v0

--- a/solution.py
+++ b/solution.py
@@ -33,7 +33,8 @@
         precision=highest,
         preferred_element_type=jnp.float32,
     )
-    small_gram = lax.psum(own_gram, ("row", "col"))
+    form_the_samples = lambda a0: lax.psum(lax.psum(a0, axis_name="col"), axis_name="row")
+    small_gram = form_the_samples(own_gram)
     factor = jnp.linalg.cholesky(small_gram)
     basis_cols = jax.scipy.linalg.solve_triangular(factor, second_image.T, lower=True).T
     block_basis = lax.all_gather(basis_cols, "col", axis=0, tiled=True)

time: 614 us -> 586 us (0.954)
  waiting for transfers between devices: 444 us -> 416 us
    psum x1 -> x2, waiting for transfers between devices: 129 us -> 101 us  [the longest x1 57.3 us: body(): lax.psum(lax.psum(a0, axis_name='col'), axis_name='row')]
  transfers between devices with their start and end apart: 8 -> 9, of which waited for: 8 -> 9; matrix products, arithmetic and copies ran while one was open for 0% -> 0% of each run, Pallas kernels for 0% -> 0%
where the time goes in v1:
time: 586 us
  waiting for transfers between devices  416 us (71%)
  matrix products  83.1 us (14%)
  other arithmetic  58 us (10%)
  between operations  15.6 us (3%)
  local copies, waits for them, and re-layouts  8.87 us (2%)
    reduce_scatter x1, waiting for transfers between devices, body(): lax.psum_scatter(lax.dot_general(gram, own_rows, contract_rows, preferred...  89.6 us
    psum x1, waiting for transfers between devices, body(): lax.psum(lax.psum(a0, axis_name='col'), axis_name='row')  57.3 us
    all_gather x1, waiting for transfers between devices, body(): block_basis = lax.all_gather(basis_cols, 'col', axis=0, tiled=True)  51.7 us
    reduce_scatter x1, waiting for transfers between devices, body(): lax.psum_scatter(jnp.dot(gram, col_rows, preferred_element_type=jnp.float...  51.5 us
    all_gather x1, waiting for transfers between devices, body(): col_rows = lax.all_gather(first_image, 'row', axis=0, tiled=True)  45.4 us
    psum x1, waiting for transfers between devices, body(): lax.psum(a0, axis_name='col')  43.2 us
    all_gather x1, waiting for transfers between devices, body(): own_rows = lax.all_gather(start_basis, 'col', axis=0, tiled=True)  39.8 us
    another operation x6, other arithmetic, body(): factor = jnp.linalg.cholesky(small_gram)  34 us
  transfers between devices with their start and end apart: 9, of which 9 were waited for; matrix products, arithmetic and copies ran while one was open for 0% of the time, Pallas kernels for 0%

profile of v1, /device:TPU:0, one launch (start us, length us, event | category | flops | bytes accessed | tf_op | source)
XLA Modules:
  0.0 585.6 jit_solution(12584499165185488492)
XLA Ops:
  7.2 0.7 all-gather.4.cloned.1.call-update
  7.9 39.8 %all-gather.4.cloned.1.call-done = bf16[4096,256]{1,0:T(8,128)(2,1)} async-done(((bf16[1024,256]{1,0:T(8,128)(2,1)}), bf16[4096,256]{1,0:T(8,128)(2,1)}) %all-gather.4.cloned.1.call-update) | async-done | bytes 2097168 | tf_op jit(solution)/shard_map/all_gather | solution.py:15
  47.8 30.0 %fusion.9 = f32[8192,256]{1,0:T(8,128)} fusion(bf16[4096,8192]{1,0:T(8,128)(2,1)} %param.3, bf16[4096,256]{1,0:T(8,128)(2,1)} %all-gather.4.cloned.1.call-done), kind=kOutput, calls=%fused_computation.32 | convolution fusion | flops 17179869184 | bytes 77594624 | tf_op jit(solution)/shard_map/dot_general | solution.py:17
  77.8 89.6 %reduce-scatter.4.cloned.1.call-done = f32[1024,256]{1,0:T(8,128)} async-done(((f32[8192,256]{1,0:T(8,128)}), f32[1024,256]{1,0:T(8,128)}) %reduce-scatter.4.cloned.1.call-update) | async-done | bytes 1048592 | tf_op jit(solution)/shard_map/reduce_scatter | solution.py:16
  167.4 2.1 convert_element_type.3
  169.6 45.4 %all-gather.6.cloned.1.call-done = bf16[8192,256]{1,0:T(8,128)(2,1)} async-done(((bf16[1024,256]{1,0:T(8,128)(2,1)}), bf16[8192,256]{1,0:T(8,128)(2,1)}) %all-gather.6.cloned.1.call-update) | async-done | bytes 4194320 | tf_op jit(solution)/shard_map/all_gather | solution.py:22
  215.0 29.2 %convolution_bitcast_fusion = f32[4096,256]{0,1:T(8,128)} fusion(bf16[8192,256]{1,0:T(8,128)(2,1)} %all-gather.6.cloned.1.call-done, bf16[4096,8192]{1,0:T(8,128)(2,1)} %param.3), kind=kOutput, calls=%fused_computation.2 | convolution fusion | flops 17179869184 | bytes 75497472 | tf_op jit(solution)/shard_map/dot_general | solution.py:24
  244.3 51.5 %reduce-scatter.6.cloned.1.call-done = f32[1024,256]{0,1:T(8,128)} async-done(((f32[4096,256]{0,1:T(8,128)}), f32[1024,256]{0,1:T(8,128)}) %reduce-scatter.6.cloned.1.call-update) | async-done | bytes 1048592 | tf_op jit(solution)/shard_map/reduce_scatter | solution.py:23
  295.8 3.4 fusion.10
  299.2 43.2 %all-reduce.4.cloned.1.call-done = f32[256,256]{0,1:T(8,128)} async-done(((f32[256,256]{0,1:T(8,128)}), f32[256,256]{0,1:T(8,128)}) %all-reduce.4.cloned.1.call-update) | async-done | bytes 262160 | tf_op jit(solution)/shard_map/psum | solution.py:36
  342.6 57.3 %all-reduce.6.cloned.1.call-done = f32[256,256]{0,1:T(8,128)} async-done(((f32[256,256]{0,1:T(8,128)}), f32[256,256]{0,1:T(8,128)}) %all-reduce.6.cloned.1.call-update) | async-done | bytes 262160 | tf_op jit(solution)/shard_map/psum | solution.py:36
  400.0 1.1 copy.6
  401.1 1.0 fusion.2
  402.1 11.7 %cholesky.50 = f32[128,128]{1,0:T(8,128)S(1)} custom-call(f32[128,128]{1,0:T(8,128)S(1)} %cholesky.118), custom_call_target="Cholesky" | custom-call | tf_op jit(solution)/shard_map/jit(cholesky)/cholesky | solution.py:38
  413.8 9.8 %custom-call.15 = f32[1,128,128]{1,2,0:T(8,128)S(1)} custom-call(f32[1,128,128]{2,1,0:T(8,128)S(1)} %get-tuple-element.25), custom_call_target="InvertDiagBlocksLowerTriangular" | custom-call | tf_op jit(solution)/shard_map/jit(cholesky)/cholesky | solution.py:38
  424.2 11.7 %cholesky.105 = f32[128,128]{1,0:T(8,128)S(1)} custom-call(f32[128,128]{1,0:T(8,128)S(1)} %convolution_subtract_fusion.1), custom_call_target="Cholesky" | custom-call | tf_op jit(solution)/shard_map/jit(cholesky)/cholesky | solution.py:38
  435.9 0.7 compare_reduce_fusion
  438.1 4.3 while.1
  438.9 1.4 bitcast_dynamic-update-slice_fusion.2
  440.9 1.4 bitcast_dynamic-update-slice_fusion.2
  442.4 19.7 %custom-call.16 = f32[2,128,128]{1,2,0:T(8,128)S(1)} custom-call(f32[2,128,128]{2,1,0:T(8,128)S(1)} %get-tuple-element.9), custom_call_target="InvertDiagBlocksLowerTriangular" | custom-call | tf_op jit(solution)/shard_map/jit(_solve_triangular)/triangular_solve | solution.py:39
  462.1 0.6 fusion
  463.3 0.6 fusion.4
  463.9 1.0 maximum_bitcast_fusion
  465.0 51.7 %all-gather.8.cloned.1.call-done = f32[4096,256]{0,1:T(8,128)} async-done(((f32[1024,256]{0,1:T(8,128)}), f32[4096,256]{0,1:T(8,128)}) %all-gather.8.cloned.1.call-update) | async-done | bytes 4194320 | tf_op jit(solution)/shard_map/all_gather | solution.py:40
  516.8 18.3 %fusion.11 = f32[256,1024]{1,0:T(8,128)} fusion(f32[4096,256]{0,1:T(8,128)} %all-gather.8.cloned.1.call-done, f32[4096,1024]{1,0:T(8,128)} %param.5), kind=kOutput, calls=%fused_computation.34 | convolution fusion | flops 12884901888 | bytes 22020096 | tf_op jit(solution)/shard_map/dot_general | solution.py:42
  535.1 32.8 %reduce-scatter.8.cloned.1.call-done = f32[32,1024]{1,0:T(8,128)} async-done(((f32[256,1024]{1,0:T(8,128)}), f32[32,1024]{1,0:T(8,128)}) %reduce-scatter.8.cloned.1.call-update) | async-done | bytes 131088 | tf_op jit(solution)/shard_map/reduce_scatter | solution.py:41
  567.8 1.6 reshape.30
  569.5 3.6 all-to-all-start
  573.2 1.3 copy.8
  574.5 3.6 all-to-all-done
  578.1 0.7 reshape.31
  (34 shorter events, 3.2 us)
Async XLA Ops:
  7.2 40.6 %all-gather.4.cloned.1.call-start = ((), (), s32[]{:S(2)}) async-start(), calls=%async_computation.4 | async-start | bytes 2621440 | tf_op jit(solution)/shard_map/all_gather | solution.py:15
  7.9 159.5 %reduce-scatter.4.cloned.1.call-start = ((), (), s32[]{:S(2)}) async-start(), calls=%async_computation.5 | async-start | bytes 9437184 | tf_op jit(solution)/shard_map/reduce_scatter | solution.py:16
  77.7 137.3 %all-gather.6.cloned.1.call-start = ((), (), s32[]{:S(2)}) async-start(), calls=%async_computation.6 | async-start | bytes 4718592 | tf_op jit(solution)/shard_map/all_gather | solution.py:22
  169.5 126.2 %reduce-scatter.6.cloned.1.call-start = ((), (), s32[]{:S(2)}) async-start(), calls=%async_computation.7 | async-start | bytes 5242880 | tf_op jit(solution)/shard_map/reduce_scatter | solution.py:23
  244.2 98.2 %all-reduce.4.cloned.1.call-start = ((), (), s32[]{:S(2)}) async-start(), calls=%async_computation.8 | async-start | bytes 524288 | tf_op jit(solution)/shard_map/psum | solution.py:36
  295.8 166.3 %copy-start = (f32[1024,256]{0,1:T(8,128)S(1)}, f32[1024,256]{0,1:T(8,128)}, u32[]{:S(2)}) copy-start(f32[1024,256]{0,1:T(8,128)} %reduce-scatter.6.cloned.1.call-done) | copy-start | bytes 3145732
  299.1 100.8 %all-reduce.6.cloned.1.call-start = ((), (), s32[]{:S(2)}) async-start(), calls=%async_computation.9 | async-start | bytes 524288 | tf_op jit(solution)/shard_map/psum | solution.py:36
  342.4 174.4 %all-gather.8.cloned.1.call-start = ((), (), s32[]{:S(2)}) async-start(), calls=%async_computation.10 | async-start | bytes 5242880 | tf_op jit(solution)/shard_map/all_gather | solution.py:40
  465.0 102.9 %reduce-scatter.8.cloned.1.call-start = ((), (), s32[]{:S(2)}) async-start(), calls=%async_computation.11 | async-start | bytes 1179648 | tf_op jit(solution)/shard_map/reduce_scatter | solution.py:41
  569.5 8.6 %all-to-all-start = ((f32[32,4,256]{2,1,0:T(4,128)}), f32[32,4,256]{2,1,0:T(4,128)S(1)}, u32[]{:S(2)}, u32[]{:S(2)}) async-start(f32[32,4,256]{2,1,0:T(4,128)} %reshape.30), calls=%async_computation.3 | async-start | bytes 262144 | tf_op jit(solution)/shard_map/all_to_all | solution.py:52
Sparse Core Ops, SparseCore 0:
  9.8 37.8 all-gather.3
  77.9 89.5 reduce-scatter.3
  169.6 45.3 all-gather.5
  244.3 51.3 reduce-scatter.5
  299.3 43.0 all-reduce.3
  344.5 55.4 all-reduce.5
  465.1 51.6 all-gather.7
  535.2 32.6 reduce-scatter.7
